TPU v7x, 32 devices: a whole 2x2x4 slice. The times are simulated.
32 devices in a mesh: dp: 16 (over z, x, core), mp: 2 (over y).
Axes of the slice: x: 2, y: 2, z: 4, core: 2. Of those that a mesh axis runs over, the one named last changes fastest.
Arguments:
- patches: bfloat16 [40960, 512], P(('dp', 'mp')), may hold values from -6 to 6
- cotangent: bfloat16 [40960, 512], P(('dp', 'mp')), may hold values from -6 to 6
- key_count: int32 [80], P('dp'), may hold values from 64 to 512, as said below
- w_qkv: float32 [3, 512, 512], P(None, None, 'mp')
- w_proj: float32 [512, 512], P('mp'), may hold values from -1 to 1
- w_up: float32 [512, 2048], P(None, 'mp')
- w_down: float32 [2048, 512], P('mp'), may hold values from -0.125 to 0.125
- qv_bias: float32 [2, 512], P(None, 'mp'), may hold values from -3 to 3
- up_bias: float32 [2048], P('mp'), may hold values from -3 to 3
- vec_params: float32 [6, 512], replicated
- first_qkv: float32 [3, 512, 512], P(None, None, 'mp'), may hold values from -0.00028163442 to 0.00028163442
- second_qkv: float32 [3, 512, 512], P(None, None, 'mp'), may hold values from 1.6815404e-08 to 6.6627074e-08
- first_proj: float32 [512, 512], P('mp'), may hold values from -0.00028163442 to 0.00028163442
- second_proj: float32 [512, 512], P('mp'), may hold values from 1.6815404e-08 to 6.6627074e-08
- first_up: float32 [512, 2048], P(None, 'mp'), may hold values from -0.00028163442 to 0.00028163442
- second_up: float32 [512, 2048], P(None, 'mp'), may hold values from 1.6815404e-08 to 6.6627074e-08
- first_down: float32 [2048, 512], P('mp'), may hold values from -0.00028163442 to 0.00028163442
- second_down: float32 [2048, 512], P('mp'), may hold values from 1.6815404e-08 to 6.6627074e-08
- first_qv_bias: float32 [2, 512], P(None, 'mp'), may hold values from -0.00056326884 to 0.00056326884
- second_qv_bias: float32 [2, 512], P(None, 'mp'), may hold values from 6.6627074e-08 to 2.665083e-07
- first_up_bias: float32 [2048], P('mp'), may hold values from -0.00056326884 to 0.00056326884
- second_up_bias: float32 [2048], P('mp'), may hold values from 9.518153e-09 to 3.8072614e-08
- first_vec: float32 [6, 512], replicated, may hold values from -0.00056326884 to 0.00056326884
- second_vec: float32 [6, 512], replicated, may hold values from 6.6627074e-08 to 2.665083e-07
Outputs:
- activations: bfloat16 [40960, 512], P(('dp', 'mp'))
- input_grad: float32 [40960, 512], P(('dp', 'mp'))
- grad_norm: float32 [], replicated
- qkv_new: float32 [3, 512, 512], P(None, None, 'mp')
- qkv_first: float32 [3, 512, 512], P(None, None, 'mp')
- qkv_second: float32 [3, 512, 512], P(None, None, 'mp')
- proj_new: float32 [512, 512], P('mp')
- proj_first: float32 [512, 512], P('mp')
- proj_second: float32 [512, 512], P('mp')
- up_new: float32 [512, 2048], P(None, 'mp')
- up_first: float32 [512, 2048], P(None, 'mp')
- up_second: float32 [512, 2048], P(None, 'mp')
- down_new: float32 [2048, 512], P('mp')
- down_first: float32 [2048, 512], P('mp')
- down_second: float32 [2048, 512], P('mp')
- qv_bias_new: float32 [2, 512], P(None, 'mp')
- qv_bias_first: float32 [2, 512], P(None, 'mp')
- qv_bias_second: float32 [2, 512], P(None, 'mp')
- up_bias_new: float32 [2048], P('mp')
- up_bias_first: float32 [2048], P('mp')
- up_bias_second: float32 [2048], P('mp')
- vec_new: float32 [6, 512], replicated
- vec_first: float32 [6, 512], replicated
- vec_second: float32 [6, 512], replicated
Inputs may be any that keep to these rules, and one draw needn't show every extreme that they name: `key_count`: each group's count is 512 (a full field) or between 64 and 512 // 4 (a small field padded); group 0 is full.
All inputs are finite; a program needn't handle non-finite values.
Results may differ from a plain program's by a relative error of at most 0.025.
Values may be sent and summed in bfloat16 or wider, within the bound.
A program may use at most 256 MiB of HBM per device.

v0:
```python
import jax
import jax.numpy as jnp
from jax import lax
from jax.sharding import PartitionSpec as P

HD = 32
ADAM_STEP = 10
NORM_EPS = 1e-06
BETA_FIRST = 0.9
BETA_SECOND = 0.95
ADAM_EPS = 1e-08
DECAY_RATE = 0.05
MATRIX_RATE = 0.1
VECTOR_RATE = 0.8
CLIP_NORM = 1.0
MASK_FILL = -1e30


def norm_forward(values, norm_gain, norm_shift):
    row_mean = jnp.mean(values, axis=-1, keepdims=True)
    centred = values - row_mean
    inverse = lax.rsqrt(jnp.mean(centred * centred, axis=-1, keepdims=True) + NORM_EPS)
    normed = centred * inverse
    return (normed * norm_gain + norm_shift, normed, inverse)


def norm_backward(grad_rows, normed, inverse, norm_gain):
    scaled = grad_rows * norm_gain
    centre_term = jnp.mean(scaled, axis=-1, keepdims=True)
    slope_term = jnp.mean(scaled * normed, axis=-1, keepdims=True)
    return inverse * (scaled - centre_term - normed * slope_term)


def exact_gelu(values):
    return jax.nn.gelu(values, approximate=False)


def key_mask(key_count, length):
    position = lax.broadcasted_iota(jnp.int32, (1, 1, 1, length), 3)
    return position < key_count[:, None, None, None]


def masked_scores(queries, key_rows, key_count):
    raw_scores = jnp.einsum(
        "sqhe,skhe->shqk", queries, key_rows, preferred_element_type=jnp.float32
    )
    scaled = raw_scores * queries.shape[-1] ** (-0.5)
    return jnp.where(key_mask(key_count, key_rows.shape[1]), scaled, MASK_FILL)


def attend_backward(queries, key_rows, value_rows, key_count, log_total, attended_grad):
    scores = masked_scores(queries, key_rows, key_count)
    probs = jnp.exp(scores - log_total)
    probs_low = probs.astype(jnp.bfloat16)
    probs_grad = jnp.einsum(
        "sqhe,skhe->shqk", attended_grad, value_rows, preferred_element_type=jnp.float32
    )
    score_grad = probs * (probs_grad - jnp.sum(probs_grad * probs, axis=-1, keepdims=True))
    visible = key_mask(key_count, key_rows.shape[1])
    raw_grad = jnp.where(visible, score_grad * queries.shape[-1] ** (-0.5), 0.0).astype(
        jnp.bfloat16
    )
    query_grad = jnp.einsum(
        "shqk,skhe->sqhe", raw_grad, key_rows, preferred_element_type=jnp.float32
    )
    key_grad = jnp.einsum("shqk,sqhe->skhe", raw_grad, queries, preferred_element_type=jnp.float32)
    value_grad = jnp.einsum(
        "shqk,sqhe->skhe", probs_low, attended_grad, preferred_element_type=jnp.float32
    )
    return jnp.stack([query_grad, key_grad, value_grad])


def own_slice(values, own_start, own_rows):
    return lax.dynamic_slice_in_dim(values, own_start, own_rows, 0)


def contract_rows(left, right):
    return lax.dot_general(
        left, right, (((0,), (0,)), ((), ())), preferred_element_type=jnp.float32
    )


def contract_cols(left, right):
    return lax.dot_general(
        left, right, (((1,), (1,)), ((), ())), preferred_element_type=jnp.float32
    )


def adam_update(weight, gradient, moment_one, moment_two, step_rate, decay_rate):
    first_new = BETA_FIRST * moment_one + (1.0 - BETA_FIRST) * gradient
    second_new = BETA_SECOND * moment_two + (1.0 - BETA_SECOND) * gradient * gradient
    first_hat = first_new / (1.0 - BETA_FIRST**ADAM_STEP)
    second_hat = second_new / (1.0 - BETA_SECOND**ADAM_STEP)
    weight_new = weight - step_rate * (
        first_hat / (jnp.sqrt(second_hat) + ADAM_EPS) + decay_rate * weight
    )
    return (weight_new, first_new, second_new)


def local(
    patches,
    cotangent,
    key_count,
    w_qkv,
    w_proj,
    w_up,
    w_down,
    qv_bias,
    up_bias,
    vec_params,
    first_qkv,
    second_qkv,
    first_proj,
    second_proj,
    first_up,
    second_up,
    first_down,
    second_down,
    first_qv_bias,
    second_qv_bias,
    first_up_bias,
    second_up_bias,
    first_vec,
    second_vec,
):
    own_rows = patches.shape[0]
    seq_count = key_count.shape[0]
    own_start = lax.axis_index("mp") * own_rows
    local_width = w_proj.shape[0]
    local_heads = local_width // HD
    own_grad = cotangent.astype(jnp.float32)
    qkv_low = w_qkv.astype(jnp.bfloat16)
    proj_low = w_proj.astype(jnp.bfloat16)
    up_low = w_up.astype(jnp.bfloat16)
    down_low = w_down.astype(jnp.bfloat16)
    gain_one, shift_one = (vec_params[0], vec_params[1])
    gain_two, shift_two = (vec_params[2], vec_params[3])
    proj_shift, down_shift = (vec_params[4], vec_params[5])
    qkv_shift = jnp.stack([qv_bias[0], jnp.zeros_like(qv_bias[0]), qv_bias[1]])[:, None, :]
    gathered, grad_all = (
        lax.all_gather(patches, "mp", axis=0, tiled=True),
        lax.all_gather(cotangent, "mp", axis=0, tiled=True),
    )
    whole_rows = gathered.astype(jnp.float32)
    normed_all, unit_one, inverse_one = norm_forward(whole_rows, gain_one, shift_one)
    norm_one = normed_all.astype(jnp.bfloat16)
    projected = (
        jnp.einsum("td,cde->cte", norm_one, qkv_low, preferred_element_type=jnp.float32) + qkv_shift
    )
    shaped = projected.astype(jnp.bfloat16).reshape(3, seq_count, -1, local_heads, HD)
    queries, key_rows, value_rows = (shaped[0], shaped[1], shaped[2])
    scores = masked_scores(queries, key_rows, key_count)
    top_score = jnp.max(scores, axis=-1, keepdims=True)
    log_total = top_score + jnp.log(jnp.sum(jnp.exp(scores - top_score), axis=-1, keepdims=True))
    probs_low = jnp.exp(scores - log_total).astype(jnp.bfloat16)
    attended = jnp.einsum(
        "shqk,skhe->sqhe", probs_low, value_rows, preferred_element_type=jnp.float32
    )
    attended_low = attended.astype(jnp.bfloat16).reshape(-1, local_width)
    proj_part = jnp.dot(attended_low, proj_low, preferred_element_type=jnp.float32)
    resid_all = whole_rows + lax.psum(proj_part, "mp") + proj_shift
    mid_all, unit_two, inverse_two = norm_forward(resid_all, gain_two, shift_two)
    norm_two = mid_all.astype(jnp.bfloat16)
    up_pre = jnp.dot(norm_two, up_low, preferred_element_type=jnp.float32) + up_bias
    hidden_full, gelu_pull = jax.vjp(exact_gelu, up_pre)
    hidden_low = hidden_full.astype(jnp.bfloat16)
    down_part = jnp.dot(hidden_low, down_low, preferred_element_type=jnp.float32)
    out_all = (
        resid_all + lax.psum(down_part.astype(jnp.bfloat16), "mp").astype(jnp.float32) + down_shift
    )
    block_out = own_slice(out_all, own_start, own_rows)
    activations = block_out.astype(jnp.bfloat16)
    down_grad = contract_rows(hidden_low, grad_all)
    hidden_grad = contract_cols(grad_all, down_low)
    up_grad_rows = gelu_pull(hidden_grad)[0].astype(jnp.bfloat16)
    up_grad = contract_rows(norm_two, up_grad_rows)
    up_bias_grad = jnp.sum(up_grad_rows.astype(jnp.float32), axis=0)
    mid_part = contract_cols(up_grad_rows, up_low)
    mid_all_grad = lax.psum(mid_part.astype(jnp.bfloat16), "mp").astype(jnp.float32)
    resid_all_grad = grad_all.astype(jnp.float32) + norm_backward(
        mid_all_grad, unit_two, inverse_two, gain_two
    )
    branch_low = resid_all_grad.astype(jnp.bfloat16)
    own_branch = own_slice(branch_low, own_start, own_rows)
    mid_grad = own_slice(mid_all_grad, own_start, own_rows)
    mid_unit = own_slice(unit_two, own_start, own_rows)
    proj_grad = contract_rows(attended_low, branch_low)
    attended_grad = (
        contract_cols(branch_low, proj_low)
        .astype(jnp.bfloat16)
        .reshape(seq_count, -1, local_heads, HD)
    )
    qkv_grads = attend_backward(queries, key_rows, value_rows, key_count, log_total, attended_grad)
    qkv_grad_rows = qkv_grads.reshape(3, -1, local_width).astype(jnp.bfloat16)
    qkv_grad = jnp.einsum(
        "td,cte->cde", norm_one, qkv_grad_rows, preferred_element_type=jnp.float32
    )
    qkv_grad_sums = jnp.sum(qkv_grad_rows.astype(jnp.float32), axis=1)
    qv_bias_grad = jnp.stack([qkv_grad_sums[0], qkv_grad_sums[2]])
    first_part = jnp.einsum(
        "cte,cde->td", qkv_grad_rows, qkv_low, preferred_element_type=jnp.float32
    )
    first_all = lax.psum(first_part.astype(jnp.bfloat16), "mp").astype(jnp.float32)
    input_all = resid_all_grad + norm_backward(first_all, unit_one, inverse_one, gain_one)
    input_grad = own_slice(input_all, own_start, own_rows)
    own_first_grad = own_slice(first_all, own_start, own_rows)
    own_unit_one = own_slice(unit_one, own_start, own_rows)
    vec_grad = jnp.stack(
        [
            jnp.sum(own_first_grad * own_unit_one, axis=0),
            jnp.sum(own_first_grad, axis=0),
            jnp.sum(mid_grad * mid_unit, axis=0),
            jnp.sum(mid_grad, axis=0),
            jnp.sum(own_branch.astype(jnp.float32), axis=0),
            jnp.sum(own_grad, axis=0),
        ]
    )
    summed = (
        lax.psum(qkv_grad.astype(jnp.bfloat16), "dp").astype(jnp.float32),
        lax.psum(proj_grad.astype(jnp.bfloat16), "dp").astype(jnp.float32),
        lax.psum(up_grad.astype(jnp.bfloat16), "dp").astype(jnp.float32),
        lax.psum(down_grad.astype(jnp.bfloat16), "dp").astype(jnp.float32),
        lax.psum(qv_bias_grad.astype(jnp.bfloat16), "dp").astype(jnp.float32),
        lax.psum(up_bias_grad.astype(jnp.bfloat16), "dp").astype(jnp.float32),
        lax.psum(vec_grad.astype(jnp.bfloat16), "dp").astype(jnp.float32),
    )
    split_square = jnp.float32(0.0)
    for gradient in summed[:6]:
        split_square = split_square + jnp.sum(gradient * gradient)
    vec_total, split_total = lax.psum((summed[6], split_square), "mp")
    grad_norm = jnp.sqrt(split_total + jnp.sum(vec_total * vec_total))
    factor = jnp.minimum(1.0, CLIP_NORM / (grad_norm + 1e-06))
    qkv_new, qkv_first, qkv_second = adam_update(
        w_qkv, summed[0] * factor, first_qkv, second_qkv, MATRIX_RATE, DECAY_RATE
    )
    proj_new, proj_first, proj_second = adam_update(
        w_proj, summed[1] * factor, first_proj, second_proj, MATRIX_RATE, DECAY_RATE
    )
    up_new, up_first, up_second = adam_update(
        w_up, summed[2] * factor, first_up, second_up, MATRIX_RATE, DECAY_RATE
    )
    down_new, down_first, down_second = adam_update(
        w_down, summed[3] * factor, first_down, second_down, MATRIX_RATE, DECAY_RATE
    )
    qvb_new, qvb_first, qvb_second = adam_update(
        qv_bias, summed[4] * factor, first_qv_bias, second_qv_bias, VECTOR_RATE, 0.0
    )
    upb_new, upb_first, upb_second = adam_update(
        up_bias, summed[5] * factor, first_up_bias, second_up_bias, VECTOR_RATE, 0.0
    )
    vec_new, vec_first, vec_second = adam_update(
        vec_params, vec_total * factor, first_vec, second_vec, VECTOR_RATE, 0.0
    )
    return (
        activations,
        input_grad,
        grad_norm,
        qkv_new,
        qkv_first,
        qkv_second,
        proj_new,
        proj_first,
        proj_second,
        up_new,
        up_first,
        up_second,
        down_new,
        down_first,
        down_second,
        qvb_new,
        qvb_first,
        qvb_second,
        upb_new,
        upb_first,
        upb_second,
        vec_new,
        vec_first,
        vec_second,
    )


def solution(mesh):
    return jax.shard_map(
        local,
        mesh=mesh,
        in_specs=(
            P(("dp", "mp"), None),
            P(("dp", "mp"), None),
            P("dp"),
            P(None, None, "mp"),
            P("mp", None),
            P(None, "mp"),
            P("mp", None),
            P(None, "mp"),
            P("mp"),
            P(),
            P(None, None, "mp"),
            P(None, None, "mp"),
            P("mp", None),
            P("mp", None),
            P(None, "mp"),
            P(None, "mp"),
            P("mp", None),
            P("mp", None),
            P(None, "mp"),
            P(None, "mp"),
            P("mp"),
            P("mp"),
            P(),
            P(),
        ),
        out_specs=(
            P(("dp", "mp"), None),
            P(("dp", "mp"), None),
            P(),
            P(None, None, "mp"),
            P(None, None, "mp"),
            P(None, None, "mp"),
            P("mp", None),
            P("mp", None),
            P("mp", None),
            P(None, "mp"),
            P(None, "mp"),
            P(None, "mp"),
            P("mp", None),
            P("mp", None),
            P("mp", None),
            P(None, "mp"),
            P(None, "mp"),
            P(None, "mp"),
            P("mp"),
            P("mp"),
            P("mp"),
            P(),
            P(),
            P(),
        ),
        check_vma=False,
    )
```

profile of v0, /device:TPU:0, one launch (start us, length us, event | category | flops | bytes accessed | tf_op | source)
XLA Modules:
  0.0 950.1 jit_solution(12365071723800339372)
XLA Ops:
  11.1 40.2 %all-gather.3.cloned.1.call-done = bf16[2560,512]{1,0:T(8,128)(2,1)} async-done(((bf16[1280,512]{1,0:T(8,128)(2,1)}), bf16[2560,512]{1,0:T(8,128)(2,1)}) %all-gather.3.cloned.1.call-update) | async-done | bytes 2621456 | tf_op jit(solution)/shard_map/all_gather | solution.py:141
  81.3 20.5 %fusion.2 = (f32[5,8,512]{2,1,0:T(8,128)S(1)}, f32[5,8,512,512]{2,3,1,0:T(8,128)}) fusion(pred[5,512]{1,0:T(8,128)(4,1)S(1)} %iota_compare_fusion, bf16[5,512,8,32]{1,0,3,2:T(8,128)(2,1)} %squeeze.11, bf16[5,512,8,32]{1,0,3,2:T(8,128)(2,1)} %squeeze.10), kind=kOutput, calls=%fused_computation.7 | convolution fusion | flops 702525440 | bytes 44648960 | tf_op jit(solution)/shard_map/sqhe,skhe->shqk/dot_general | solution.py:44
  101.7 17.9 %exponential_reduce_fusion = f32[5,8,512]{2,1,0:T(8,128)S(1)} fusion(f32[5,8,512,512]{2,3,1,0:T(8,128)} %get-tuple-element.135, f32[5,8,512]{2,1,0:T(8,128)S(1)} %get-tuple-element.134, pred[5,512]{1,0:T(8,128)(4,1)S(1)} %iota_compare_fusion), kind=kLoop, calls=%fused_computation.5 | loop fusion | flops 41922560 | bytes 42109440 | tf_op jit(solution)/shard_map/reduce_sum | solution.py:154
  119.7 19.6 %fusion.64 = bf16[5,512,8,32]{1,3,2,0:T(8,128)(2,1)} fusion(bf16[5,512,8,32]{1,0,3,2:T(8,128)(2,1)} %squeeze.9, f32[5,8,512,512]{2,3,1,0:T(8,128)} %get-tuple-element.135, f32[5,8,512]{2,1,0:T(8,128)S(1)} %log_add_fusion, pred[5,512]{1,0:T(8,128)(4,1)S(1)} %iota_compare_fusion), kind=kOutput, calls=%fused_computation.103 | convolution fusion | flops 713687040 | bytes 44648960 | tf_op jit(solution)/shard_map/shqk,skhe->sqhe/dot_general | solution.py:156
  147.2 129.9 %all-reduce.9.cloned.1.call-done = f32[2560,512]{1,0:T(8,128)} async-done(((f32[2560,512]{1,0:T(8,128)}), f32[2560,512]{1,0:T(8,128)}) %all-reduce.9.cloned.1.call-update) | async-done | bytes 5242896 | tf_op jit(solution)/shard_map/psum | solution.py:161
  285.3 26.6 %multiply_convert_fusion = (bf16[2560,1024]{1,0:T(8,128)(2,1)}, f32[2560,1024]{1,0:T(8,128)}, f32[2560,1024]{1,0:T(8,128)}) fusion(f32[1024]{0:T(1024)S(1)} %copy-done.48, f32[512,1024]{1,0:T(8,128)S(1)} %copy-done.29, f32[2560,512]{1,0:T(8,128)S(1)} %subtract_multiply_fusion, f32[512]{0:T(512)S(1)} %bitcast.72, f32[512]{0:T(512)S(1)} %bitcast.61), kind=kOutput, calls=%fused_computation.24 | convolution fusion | flops 2861826048 | bytes 33562624 | tf_op jit(solution)/shard_map/dot_general | solution.py:164
  311.9 5.8 all-gather.5.cloned.1.call-done
  317.8 12.5 %fusion.149 = (bf16[1024]{0:T(1024)(128)(2,1)}, bf16[2560,1024]{1,0:T(8,128)(2,1)S(1)}) fusion(f32[2560,1024]{1,0:T(8,128)} %get-tuple-element.113, bf16[2560,512]{1,0:T(8,128)(2,1)} %all-gather.5.cloned.1.call-done, f32[1024,512]{1,0:T(8,128)S(1)} %copy-done.25, f32[2560,1024]{1,0:T(8,128)} %get-tuple-element.136, f32[1024]{0:T(1024)S(1)} %copy-done.48), kind=kOutput, calls=%fused_computation.190 | convolution fusion | flops 2726820864 | bytes 30939136 | tf_op jit(solution)/shard_map/dot_general | solution.py:84
  337.2 7.3 convolution_convert_fusion.5
  344.5 6.4 convolution_convert_fusion.6
  350.8 60.7 %all-reduce.11.cloned.1.call-done = bf16[2560,512]{1,0:T(8,128)(2,1)} async-done(((bf16[2560,512]{1,0:T(8,128)(2,1)}), bf16[2560,512]{1,0:T(8,128)(2,1)}) %all-reduce.11.cloned.1.call-update) | async-done | bytes 2621456 | tf_op jit(solution)/shard_map/psum | solution.py:179
  411.6 5.1 multiply_reduce_fusion.4
  416.7 6.5 fusion.142
  427.9 16.6 %fusion.65 = bf16[5,512,8,32]{1,3,2,0:T(8,128)(2,1)S(1)} fusion(bf16[5,512,8,32]{1,0,3,2:T(8,128)(2,1)S(1)} %reshape.145, f32[5,8,512,512]{2,3,1,0:T(8,128)} %get-tuple-element.135, f32[5,8,512]{2,1,0:T(8,128)S(1)} %log_add_fusion, pred[5,512]{1,0:T(8,128)(4,1)S(1)} %iota_compare_fusion), kind=kOutput, calls=%fused_computation.104 | convolution fusion | flops 713687040 | bytes 44648960 | tf_op jit(solution)/shard_map/shqk,sqhe->skhe/dot_general | solution.py:67
  444.6 16.2 %fusion.75 = f32[5,8,512,512]{2,3,1,0:T(8,128)} fusion(bf16[5,512,8,32]{1,0,3,2:T(8,128)(2,1)S(1)} %reshape.145, bf16[5,512,8,32]{1,0,3,2:T(8,128)(2,1)S(1)} %copy-done.13), kind=kOutput, calls=%fused_computation.114 | convolution fusion | flops 671088640 | bytes 44564480 | tf_op jit(solution)/shard_map/sqhe,skhe->shqk/dot_general | solution.py:55
  460.8 54.2 %fusion.69 = bf16[5,512,8,32]{1,3,2,0:T(8,128)(2,1)} fusion(f32[5,8,512,512]{2,3,1,0:T(8,128)} %fusion.75, f32[5,8,512,512]{2,3,1,0:T(8,128)} %get-tuple-element.135, f32[5,8,512]{2,1,0:T(8,128)S(1)} %log_add_fusion, pred[5,512]{1,0:T(8,128)(4,1)S(1)} %iota_compare_fusion, bf16[5,512,8,32]{1,0,3,2:T(8,128)(2,1)} %squeeze.11), kind=kOutput, calls=%fused_computation.106 | convolution fusion | flops 797594112 | bytes 86592000 | tf_op jit(solution)/shard_map/shqk,skhe->sqhe/dot_general | solution.py:63
  515.0 53.4 %fusion.66 = bf16[5,512,8,32]{1,3,2,0:T(8,128)(2,1)} fusion(f32[5,8,512,512]{2,3,1,0:T(8,128)} %fusion.75, f32[5,8,512,512]{2,3,1,0:T(8,128)} %get-tuple-element.135, f32[5,8,512]{2,1,0:T(8,128)S(1)} %log_add_fusion, pred[5,512]{1,0:T(8,128)(4,1)S(1)} %iota_compare_fusion, bf16[5,512,8,32]{1,0,3,2:T(8,128)(2,1)S(1)} %copy-done.9), kind=kOutput, calls=%fused_computation.105 | convolution fusion | flops 797594112 | bytes 86592000 | tf_op jit(solution)/shard_map/shqk,sqhe->skhe/dot_general | solution.py:66
  587.9 5.6 fusion.73
  593.6 7.7 convolution_convert_fusion.1
  622.9 74.7 %all-reduce.13.cloned.1.call-done = (bf16[3,512,256]{1,2,0:T(8,128)(2,1)}, bf16[256,512]{1,0:T(8,128)(2,1)}, bf16[512,1024]{1,0:T(8,128)(2,1)}, bf16[1024,512]{1,0:T(8,128)(2,1)}) async-done(((bf16[3,512,256]{1,2,0:T(8,128)(2,1)}, bf16[256,512]{1,0:T(8,128)(2,1)}, bf16[512,1024]{1,0:T(8,128)(2,1)}, bf16[1024,512]{1,0:T(8,128)(2,1)}), (bf16[3,512,256]{1,2,0:T(8,128)(2,1)}, bf16[256,512]{1,0:T(8,128)(2,1)}, ...) | async-done | bytes 3145744 | tf_op jit(solution)/shard_map/psum | solution.py:219
  708.8 121.4 %all-reduce.15.cloned.1.call-done = (bf16[2560,512]{1,0:T(8,128)(2,1)}, bf16[2560,512]{1,0:T(8,128)(2,1)}) async-done(((bf16[2560,512]{1,0:T(8,128)(2,1)}, bf16[2560,512]{1,0:T(8,128)(2,1)}), (bf16[2560,512]{1,0:T(8,128)(2,1)}, bf16[2560,512]{1,0:T(8,128)(2,1)})) %all-reduce.15.cloned.1.call-update) | async-done | bytes 5242896 | tf_op jit(solution)/shard_map/psum | solution.py:203
  838.0 61.2 %all-reduce.1 = (bf16[6,512]{1,0:T(8,128)(2,1)S(1)}, bf16[2,256]{1,0:T(2,128)(2,1)S(1)}, bf16[1024]{0:T(1024)(128)(2,1)S(1)}) all-reduce(bf16[6,512]{1,0:T(8,128)(2,1)S(1)} %stack.59, bf16[2,256]{1,0:T(2,128)(2,1)S(1)} %pad_maximum_fusion.2, bf16[1024]{0:T(1024)(128)(2,1)S(1)} %copy-done.56), channel_id=1, replica_groups=mesh['dp'=16,'mp'=2] {'dp'}, use_global_device_ids=true, to_apply=%region_36.37 | all-reduce | flops 4608 | bytes 18432 | tf_op jit(solution)/shard_map/psum | solution.py:225
  901.7 7.8 all-reduce
  911.5 4.7 multiply_subtract_fusion.2
  (222 shorter events, 146.0 us)
Async XLA Ops:
  7.2 44.1 %all-gather.3.cloned.1.call-start = ((), (), s32[]{:S(2)}) async-start(), calls=%async_computation | async-start | bytes 3932160 | tf_op jit(solution)/shard_map/all_gather | solution.py:141
  7.9 269.2 %all-reduce.9.cloned.1.call-start = ((), (), s32[]{:S(2)}) async-start(), calls=%async_computation.1 | async-start | bytes 10485760 | tf_op jit(solution)/shard_map/psum | solution.py:161
  11.1 48.6 %copy-start.45 = (f32[1,512]{1,0:T(1,128)}, f32[1,512]{1,0:T(1,128)S(1)}, u32[]{:S(2)}) copy-start(f32[1,512]{1,0:T(1,128)S(1)} %get-tuple-element.128) | copy-start | bytes 6148
  11.1 48.6 %copy-start.54 = (f32[1,512]{1,0:T(1,128)}, f32[1,512]{1,0:T(1,128)S(1)}, u32[]{:S(2)}) copy-start(f32[1,512]{1,0:T(1,128)S(1)} %get-tuple-element.127) | copy-start | bytes 6148
  146.4 171.4 %all-gather.5.cloned.1.call-start = ((), (), s32[]{:S(2)}) async-start(), calls=%async_computation.2 | async-start | bytes 3932160 | tf_op jit(solution)/shard_map/all_gather | solution.py:142
  147.1 264.4 %all-reduce.11.cloned.1.call-start = ((), (), s32[]{:S(2)}) async-start(), calls=%async_computation.3 | async-start | bytes 5242880 | tf_op jit(solution)/shard_map/psum | solution.py:179
  285.3 32.4 %copy-start.25 = (f32[1024,512]{1,0:T(8,128)S(1)}, f32[1024,512]{1,0:T(8,128)}, u32[]{:S(2)}) copy-start(f32[1024,512]{1,0:T(8,128)} %param.30) | copy-start | bytes 6291460
  317.8 14.9 %copy-start.30 = (f32[512,1024]{1,0:T(8,128)S(1)}, f32[512,1024]{1,0:T(8,128)}, u32[]{:S(2)}) copy-start(f32[512,1024]{1,0:T(8,128)} %param.29) | copy-start | bytes 6291460
  337.1 360.6 %all-reduce.13.cloned.1.call-start = ((), (), s32[]{:S(2)}) async-start(), calls=%async_computation.4 | async-start | bytes 6291456 | tf_op jit(solution)/shard_map/psum | solution.py:219
  350.8 65.8 %copy-start.24 = (bf16[2560,512]{1,0:T(8,128)(2,1)S(1)}, bf16[2560,512]{1,0:T(8,128)(2,1)}, u32[]{:S(2)}) copy-start(bf16[2560,512]{1,0:T(8,128)(2,1)} %all-gather.5.cloned.1.call-done) | copy-start | bytes 7864324
  427.9 16.6 %copy-start.13 = (bf16[5,512,8,32]{1,0,3,2:T(8,128)(2,1)S(1)}, bf16[5,512,8,32]{1,0,3,2:T(8,128)(2,1)}, u32[]{:S(2)}) copy-start(bf16[5,512,8,32]{1,0,3,2:T(8,128)(2,1)} %squeeze.9) | copy-start | bytes 3932164
  460.8 54.2 %copy-start.9 = (bf16[5,512,8,32]{1,0,3,2:T(8,128)(2,1)S(1)}, bf16[5,512,8,32]{1,0,3,2:T(8,128)(2,1)}, u32[]{:S(2)}) copy-start(bf16[5,512,8,32]{1,0,3,2:T(8,128)(2,1)} %squeeze.10) | copy-start | bytes 3932164
  577.5 10.4 %copy-start.2 = (bf16[2560,512]{1,0:T(8,128)(2,1)S(1)}, bf16[2560,512]{1,0:T(8,128)(2,1)}, u32[]{:S(2)}) copy-start(bf16[2560,512]{1,0:T(8,128)(2,1)} %all-gather.3.cloned.1.call-done) | copy-start | bytes 7864324
  577.5 10.4 %copy-start.38 = (f32[2560]{0:T(1024)S(1)}, f32[2560]{0:T(1024)}, u32[]{:S(2)}) copy-start(f32[2560]{0:T(1024)} %copy-done.37) | copy-start | bytes 30724
  577.5 10.4 %copy-start.40 = (f32[2560]{0:T(1024)S(1)}, f32[2560]{0:T(1024)}, u32[]{:S(2)}) copy-start(f32[2560]{0:T(1024)} %copy-done.39) | copy-start | bytes 30724
  577.5 10.4 %copy-start.46 = (f32[1,512]{1,0:T(1,128)S(1)}, f32[1,512]{1,0:T(1,128)}, u32[]{:S(2)}) copy-start(f32[1,512]{1,0:T(1,128)} %copy-done.45) | copy-start | bytes 6148
  577.5 10.4 %copy-start.55 = (f32[1,512]{1,0:T(1,128)S(1)}, f32[1,512]{1,0:T(1,128)}, u32[]{:S(2)}) copy-start(f32[1,512]{1,0:T(1,128)} %copy-done.54) | copy-start | bytes 6148
  593.5 236.7 %all-reduce.15.cloned.1.call-start = ((), (), s32[]{:S(2)}) async-start(), calls=%async_computation.5 | async-start | bytes 10485760 | tf_op jit(solution)/shard_map/psum | solution.py:203
  835.5 76.0 %copy-start.10 = (f32[3,512,256]{1,2,0:T(8,128)S(1)}, f32[3,512,256]{1,2,0:T(8,128)}, u32[]{:S(2)}) copy-start(f32[3,512,256]{1,2,0:T(8,128)} %copy.95) | copy-start | bytes 4718596
  835.6 76.0 %copy-start.11 = (f32[3,512,256]{1,2,0:T(8,128)S(1)}, f32[3,512,256]{1,2,0:T(8,128)}, u32[]{:S(2)}) copy-start(f32[3,512,256]{1,2,0:T(8,128)} %copy.92) | copy-start | bytes 4718596
  919.4 9.8 %copy-start.41 = (f32[6,512]{1,0:T(8,128)S(1)}, f32[6,512]{1,0:T(8,128)}, u32[]{:S(2)}) copy-start(f32[6,512]{1,0:T(8,128)} %param.33) | copy-start | bytes 36868
  919.4 10.4 %copy-start.21 = (f32[256,512]{1,0:T(8,128)S(1)}, f32[256,512]{1,0:T(8,128)}, u32[]{:S(2)}) copy-start(f32[256,512]{1,0:T(8,128)} %param.28) | copy-start | bytes 1572868
  919.5 10.4 %copy-start.36 = (bf16[256,512]{1,0:T(8,128)(2,1)S(1)}, bf16[256,512]{1,0:T(8,128)(2,1)}, u32[]{:S(2)}) copy-start(bf16[256,512]{1,0:T(8,128)(2,1)} %get-tuple-element.86) | copy-start | bytes 786436
  922.6 9.9 %copy-start.23 = (bf16[1024,512]{1,0:T(8,128)(2,1)S(1)}, bf16[1024,512]{1,0:T(8,128)(2,1)}, u32[]{:S(2)}) copy-start(bf16[1024,512]{1,0:T(8,128)(2,1)} %get-tuple-element.88) | copy-start | bytes 3145732
  (44 other events, 257.0 us)
Sparse Core Ops, SparseCore 0:
  9.6 41.7 all-gather.2
  146.5 130.5 all-reduce.8
  278.7 39.0 all-gather.4
  337.2 74.3 all-reduce.10
  593.6 104.0 all-reduce.12
  700.6 129.5 all-reduce.14
where the time goes:
time: 961 us; the launch traced here: 950 us
  waiting for transfers between devices  434 us (45%)
  matrix products  263 us (27%)
  other arithmetic  88.8 us (9%)
  local copies, waits for them, and re-layouts  73 us (8%)
  blocking collectives  69.1 us (7%)
  between operations  21.5 us (2%)
    psum x1, waiting for transfers between devices, local(): resid_all = whole_rows + lax.psum(proj_part, 'mp') + proj_shift  130 us
    psum x1, waiting for transfers between devices, local(): lax.psum(first_part.astype(jnp.bfloat16), 'mp').astype(jnp.float32)  121 us
    psum x1, waiting for transfers between devices, local(): lax.psum(qkv_grad.astype(jnp.bfloat16), 'dp').astype(jnp.float32)  74.7 us
    psum x1, blocking collectives, local(): lax.psum(vec_grad.astype(jnp.bfloat16), 'dp').astype(jnp.float32)  61.2 us
    psum x1, waiting for transfers between devices, local(): lax.psum(mid_part.astype(jnp.bfloat16), 'mp').astype(jnp.float32)  60.7 us
    dot_general x1, matrix products, attend_backward(): jnp.einsum('shqk,skhe->sqhe', raw_grad, key_rows, preferred_element_type=...  54.2 us
    dot_general x1, matrix products, attend_backward(): jnp.einsum('shqk,sqhe->skhe', raw_grad, queries, preferred_element_type=j...  53.4 us
    all_gather x1, waiting for transfers between devices, local(): lax.all_gather(patches, 'mp', axis=0, tiled=True)  40.2 us
  transfers between devices with their start and end apart: 6, of which 6 were waited for; matrix products, arithmetic and copies ran while one was open for 9% of the time, Pallas kernels for 0%

commit v1 on v0

--- a/solution.py
+++ b/solution.py
@@ -200,7 +200,9 @@
     first_part = jnp.einsum(
         "cte,cde->td", qkv_grad_rows, qkv_low, preferred_element_type=jnp.float32
     )
-    first_all = lax.psum(first_part.astype(jnp.bfloat16), "mp").astype(jnp.float32)
+    first_all = jnp.sum(lax.all_gather(first_part.astype(jnp.bfloat16), "mp"), axis=0).astype(
+        jnp.float32
+    )
     input_all = resid_all_grad + norm_backward(first_all, unit_one, inverse_one, gain_one)
     input_grad = own_slice(input_all, own_start, own_rows)
     own_first_grad = own_slice(first_all, own_start, own_rows)

time: 961 us -> 960 us (level)
    psum x1 -> x0, waiting for transfers between devices: 121 us -> none  [local(): lax.psum(first_part.astype(jnp.bfloat16), 'mp').astype(jnp.float32)]
    all_gather x0 -> x1, waiting for transfers between devices: none -> 57.9 us  [local(): lax.all_gather(first_part.astype(jnp.bfloat16), 'mp')]
    psum x1, waiting for transfers between devices: 60.7 us -> 115 us  [local(): lax.psum(mid_part.astype(jnp.bfloat16), 'mp').astype(jnp.float32)]
    unnamed x131 -> x123, local copies, waits for them, and re-layouts: 25 us -> 24.4 us
where the time goes in v1:
time: 960 us; the launch traced here: 950 us
  waiting for transfers between devices  429 us (45%)
  matrix products  263 us (27%)
  other arithmetic  94.1 us (10%)
  local copies, waits for them, and re-layouts  72.5 us (8%)
  blocking collectives  69.1 us (7%)
  between operations  21.5 us (2%)
    psum x1, waiting for transfers between devices, local(): resid_all = whole_rows + lax.psum(proj_part, 'mp') + proj_shift  130 us
    psum x1, waiting for transfers between devices, local(): lax.psum(mid_part.astype(jnp.bfloat16), 'mp').astype(jnp.float32)  115 us
    psum x1, waiting for transfers between devices, local(): lax.psum(qkv_grad.astype(jnp.bfloat16), 'dp').astype(jnp.float32)  78.2 us
    psum x1, blocking collectives, local(): lax.psum(vec_grad.astype(jnp.bfloat16), 'dp').astype(jnp.float32)  61.2 us
    all_gather x1, waiting for transfers between devices, local(): lax.all_gather(first_part.astype(jnp.bfloat16), 'mp')  57.9 us
    dot_general x1, matrix products, attend_backward(): jnp.einsum('shqk,skhe->sqhe', raw_grad, key_rows, preferred_element_type=...  54.4 us
    dot_general x1, matrix products, attend_backward(): jnp.einsum('shqk,sqhe->skhe', raw_grad, queries, preferred_element_type=j...  53.5 us
    all_gather x1, waiting for transfers between devices, local(): lax.all_gather(patches, 'mp', axis=0, tiled=True)  40.2 us
  transfers between devices with their start and end apart: 6, of which 6 were waited for; matrix products, arithmetic and copies ran while one was open for 9% of the time, Pallas kernels for 0%

profile of v1, /device:TPU:0, one launch (start us, length us, event | category | flops | bytes accessed | tf_op | source)
XLA Modules:
  0.0 949.6 jit_solution(5355681546725488832)
XLA Ops:
  11.1 40.2 %all-gather.5.cloned.1.call-done = bf16[2560,512]{1,0:T(8,128)(2,1)} async-done(((bf16[1280,512]{1,0:T(8,128)(2,1)}), bf16[2560,512]{1,0:T(8,128)(2,1)}) %all-gather.5.cloned.1.call-update) | async-done | bytes 2621456 | tf_op jit(solution)/shard_map/all_gather | solution.py:141
  81.3 20.5 %fusion.2 = (f32[5,8,512]{2,1,0:T(8,128)S(1)}, f32[5,8,512,512]{2,3,1,0:T(8,128)}) fusion(pred[5,512]{1,0:T(8,128)(4,1)S(1)} %iota_compare_fusion, bf16[5,512,8,32]{1,0,3,2:T(8,128)(2,1)} %squeeze.11, bf16[5,512,8,32]{1,0,3,2:T(8,128)(2,1)} %squeeze.10), kind=kOutput, calls=%fused_computation.7 | convolution fusion | flops 702525440 | bytes 44648960 | tf_op jit(solution)/shard_map/sqhe,skhe->shqk/dot_general | solution.py:44
  101.8 17.9 %exponential_reduce_fusion = f32[5,8,512]{2,1,0:T(8,128)S(1)} fusion(f32[5,8,512,512]{2,3,1,0:T(8,128)} %get-tuple-element.135, f32[5,8,512]{2,1,0:T(8,128)S(1)} %get-tuple-element.134, pred[5,512]{1,0:T(8,128)(4,1)S(1)} %iota_compare_fusion), kind=kLoop, calls=%fused_computation.5 | loop fusion | flops 41922560 | bytes 42109440 | tf_op jit(solution)/shard_map/reduce_sum | solution.py:154
  119.7 19.6 %fusion.64 = bf16[5,512,8,32]{1,3,2,0:T(8,128)(2,1)} fusion(bf16[5,512,8,32]{1,0,3,2:T(8,128)(2,1)} %squeeze.9, f32[5,8,512,512]{2,3,1,0:T(8,128)} %get-tuple-element.135, f32[5,8,512]{2,1,0:T(8,128)S(1)} %log_add_fusion, pred[5,512]{1,0:T(8,128)(4,1)S(1)} %iota_compare_fusion), kind=kOutput, calls=%fused_computation.103 | convolution fusion | flops 713687040 | bytes 44648960 | tf_op jit(solution)/shard_map/shqk,skhe->sqhe/dot_general | solution.py:156
  147.2 129.9 %all-reduce.8.cloned.1.call-done = f32[2560,512]{1,0:T(8,128)} async-done(((f32[2560,512]{1,0:T(8,128)}), f32[2560,512]{1,0:T(8,128)}) %all-reduce.8.cloned.1.call-update) | async-done | bytes 5242896 | tf_op jit(solution)/shard_map/psum | solution.py:161
  285.4 26.6 %multiply_convert_fusion = (bf16[2560,1024]{1,0:T(8,128)(2,1)}, f32[2560,1024]{1,0:T(8,128)}, f32[2560,1024]{1,0:T(8,128)}) fusion(f32[1024]{0:T(1024)S(1)} %copy-done.43, f32[512,1024]{1,0:T(8,128)S(1)} %copy-done.24, f32[2560,512]{1,0:T(8,128)S(1)} %subtract_multiply_fusion, f32[512]{0:T(512)S(1)} %bitcast.74, f32[512]{0:T(512)S(1)} %bitcast.63), kind=kOutput, calls=%fused_computation.24 | convolution fusion | flops 2861826048 | bytes 33562624 | tf_op jit(solution)/shard_map/dot_general | solution.py:164
  311.9 5.9 all-gather.7.cloned.1.call-done
  317.8 12.5 %fusion.149 = (bf16[1024]{0:T(1024)(128)(2,1)}, bf16[2560,1024]{1,0:T(8,128)(2,1)S(1)}) fusion(f32[2560,1024]{1,0:T(8,128)} %get-tuple-element.115, bf16[2560,512]{1,0:T(8,128)(2,1)} %all-gather.7.cloned.1.call-done, f32[1024,512]{1,0:T(8,128)S(1)} %copy-done.23, f32[2560,1024]{1,0:T(8,128)} %get-tuple-element.136, f32[1024]{0:T(1024)S(1)} %copy-done.43), kind=kOutput, calls=%fused_computation.190 | convolution fusion | flops 2726820864 | bytes 30939136 | tf_op jit(solution)/shard_map/dot_general | solution.py:84
  341.5 6.4 convolution_convert_fusion.5
  347.9 7.9 convolution_convert_fusion.6
  355.8 115.1 %all-reduce.12.cloned.1.call-done = (bf16[2560,512]{1,0:T(8,128)(2,1)}, bf16[2560,512]{1,0:T(8,128)(2,1)}) async-done(((bf16[2560,512]{1,0:T(8,128)(2,1)}, bf16[2560,512]{1,0:T(8,128)(2,1)}), (bf16[2560,512]{1,0:T(8,128)(2,1)}, bf16[2560,512]{1,0:T(8,128)(2,1)})) %all-reduce.12.cloned.1.call-update) | async-done | bytes 5242896 | tf_op jit(solution)/shard_map/psum | solution.py:179
  475.8 6.5 fusion.141
  487.0 16.6 %fusion.65 = bf16[5,512,8,32]{1,3,2,0:T(8,128)(2,1)S(1)} fusion(bf16[5,512,8,32]{1,0,3,2:T(8,128)(2,1)S(1)} %reshape.145, f32[5,8,512,512]{2,3,1,0:T(8,128)} %get-tuple-element.135, f32[5,8,512]{2,1,0:T(8,128)S(1)} %log_add_fusion, pred[5,512]{1,0:T(8,128)(4,1)S(1)} %iota_compare_fusion), kind=kOutput, calls=%fused_computation.104 | convolution fusion | flops 713687040 | bytes 44648960 | tf_op jit(solution)/shard_map/shqk,sqhe->skhe/dot_general | solution.py:67
  503.6 16.2 %fusion.75 = f32[5,8,512,512]{2,3,1,0:T(8,128)} fusion(bf16[5,512,8,32]{1,0,3,2:T(8,128)(2,1)S(1)} %reshape.145, bf16[5,512,8,32]{1,0,3,2:T(8,128)(2,1)S(1)} %copy-done.14), kind=kOutput, calls=%fused_computation.114 | convolution fusion | flops 671088640 | bytes 44564480 | tf_op jit(solution)/shard_map/sqhe,skhe->shqk/dot_general | solution.py:55
  519.8 54.4 %fusion.69 = bf16[5,512,8,32]{1,3,2,0:T(8,128)(2,1)} fusion(f32[5,8,512,512]{2,3,1,0:T(8,128)} %fusion.75, f32[5,8,512,512]{2,3,1,0:T(8,128)} %get-tuple-element.135, f32[5,8,512]{2,1,0:T(8,128)S(1)} %log_add_fusion, pred[5,512]{1,0:T(8,128)(4,1)S(1)} %iota_compare_fusion, bf16[5,512,8,32]{1,0,3,2:T(8,128)(2,1)} %squeeze.11), kind=kOutput, calls=%fused_computation.106 | convolution fusion | flops 797594112 | bytes 86592000 | tf_op jit(solution)/shard_map/shqk,skhe->sqhe/dot_general | solution.py:63
  574.2 53.5 %fusion.66 = bf16[5,512,8,32]{1,3,2,0:T(8,128)(2,1)} fusion(f32[5,8,512,512]{2,3,1,0:T(8,128)} %fusion.75, f32[5,8,512,512]{2,3,1,0:T(8,128)} %get-tuple-element.135, f32[5,8,512]{2,1,0:T(8,128)S(1)} %log_add_fusion, pred[5,512]{1,0:T(8,128)(4,1)S(1)} %iota_compare_fusion, bf16[5,512,8,32]{1,0,3,2:T(8,128)(2,1)S(1)} %copy-done.10), kind=kOutput, calls=%fused_computation.105 | convolution fusion | flops 797594112 | bytes 86592000 | tf_op jit(solution)/shard_map/shqk,sqhe->skhe/dot_general | solution.py:66
  647.2 5.6 fusion.73
  652.9 6.3 bitcast_convert_fusion
  678.8 78.2 %all-reduce.10.cloned.1.call-done = (bf16[3,512,256]{1,2,0:T(8,128)(2,1)}, bf16[256,512]{1,0:T(8,128)(2,1)}, bf16[512,1024]{1,0:T(8,128)(2,1)}, bf16[1024,512]{1,0:T(8,128)(2,1)}) async-done(((bf16[3,512,256]{1,2,0:T(8,128)(2,1)}, bf16[256,512]{1,0:T(8,128)(2,1)}, bf16[512,1024]{1,0:T(8,128)(2,1)}, bf16[1024,512]{1,0:T(8,128)(2,1)}), (bf16[3,512,256]{1,2,0:T(8,128)(2,1)}, bf16[256,512]{1,0:T(8,128)(2,1)}, ...) | async-done | bytes 3145744 | tf_op jit(solution)/shard_map/psum | solution.py:221
  768.4 57.9 %all-gather.9.cloned.1.call-done = bf16[5120,512]{1,0:T(8,128)(2,1)} async-done(((bf16[2560,512]{1,0:T(8,128)(2,1)}), bf16[5120,512]{1,0:T(8,128)(2,1)}) %all-gather.9.cloned.1.call-update) | async-done | bytes 5242896 | tf_op jit(solution)/shard_map/all_gather | solution.py:203
  826.3 5.7 reduce_sum.248
  839.8 61.2 %all-reduce.1 = (bf16[6,512]{1,0:T(8,128)(2,1)S(1)}, bf16[2,256]{1,0:T(2,128)(2,1)S(1)}, bf16[1024]{0:T(1024)(128)(2,1)S(1)}) all-reduce(bf16[6,512]{1,0:T(8,128)(2,1)S(1)} %stack.59, bf16[2,256]{1,0:T(2,128)(2,1)S(1)} %pad_maximum_fusion.2, bf16[1024]{0:T(1024)(128)(2,1)S(1)} %copy-done.51), channel_id=1, replica_groups=mesh['dp'=16,'mp'=2] {'dp'}, use_global_device_ids=true, to_apply=%region_36.37 | all-reduce | flops 4608 | bytes 18432 | tf_op jit(solution)/shard_map/psum | solution.py:227
  903.5 7.8 all-reduce
  930.6 6.8 multiply_subtract_fusion
  (215 shorter events, 148.9 us)
Async XLA Ops:
  7.2 44.1 %all-gather.5.cloned.1.call-start = ((), (), s32[]{:S(2)}) async-start(), calls=%async_computation | async-start | bytes 3932160 | tf_op jit(solution)/shard_map/all_gather | solution.py:141
  7.9 269.2 %all-reduce.8.cloned.1.call-start = ((), (), s32[]{:S(2)}) async-start(), calls=%async_computation.1 | async-start | bytes 10485760 | tf_op jit(solution)/shard_map/psum | solution.py:161
  11.1 48.6 %copy-start.40 = (f32[1,512]{1,0:T(1,128)}, f32[1,512]{1,0:T(1,128)S(1)}, u32[]{:S(2)}) copy-start(f32[1,512]{1,0:T(1,128)S(1)} %get-tuple-element.128) | copy-start | bytes 6148
  11.1 48.6 %copy-start.49 = (f32[1,512]{1,0:T(1,128)}, f32[1,512]{1,0:T(1,128)S(1)}, u32[]{:S(2)}) copy-start(f32[1,512]{1,0:T(1,128)S(1)} %get-tuple-element.127) | copy-start | bytes 6148
  146.4 171.4 %all-gather.7.cloned.1.call-start = ((), (), s32[]{:S(2)}) async-start(), calls=%async_computation.2 | async-start | bytes 3932160 | tf_op jit(solution)/shard_map/all_gather | solution.py:142
  147.2 323.7 %all-reduce.12.cloned.1.call-start = ((), (), s32[]{:S(2)}) async-start(), calls=%async_computation.5 | async-start | bytes 10485760 | tf_op jit(solution)/shard_map/psum | solution.py:179
  285.4 32.4 %copy-start.23 = (f32[1024,512]{1,0:T(8,128)S(1)}, f32[1024,512]{1,0:T(8,128)}, u32[]{:S(2)}) copy-start(f32[1024,512]{1,0:T(8,128)} %param.30) | copy-start | bytes 6291460
  317.8 12.5 %copy-start.25 = (f32[512,1024]{1,0:T(8,128)S(1)}, f32[512,1024]{1,0:T(8,128)}, u32[]{:S(2)}) copy-start(f32[512,1024]{1,0:T(8,128)} %param.29) | copy-start | bytes 6291460
  339.8 417.3 %all-reduce.10.cloned.1.call-start = ((), (), s32[]{:S(2)}) async-start(), calls=%async_computation.4 | async-start | bytes 6291456 | tf_op jit(solution)/shard_map/psum | solution.py:221
  487.0 16.6 %copy-start.14 = (bf16[5,512,8,32]{1,0,3,2:T(8,128)(2,1)S(1)}, bf16[5,512,8,32]{1,0,3,2:T(8,128)(2,1)}, u32[]{:S(2)}) copy-start(bf16[5,512,8,32]{1,0,3,2:T(8,128)(2,1)} %squeeze.9) | copy-start | bytes 3932164
  519.8 54.4 %copy-start.10 = (bf16[5,512,8,32]{1,0,3,2:T(8,128)(2,1)S(1)}, bf16[5,512,8,32]{1,0,3,2:T(8,128)(2,1)}, u32[]{:S(2)}) copy-start(bf16[5,512,8,32]{1,0,3,2:T(8,128)(2,1)} %squeeze.10) | copy-start | bytes 3932164
  636.8 10.4 %copy-start.2 = (bf16[2560,512]{1,0:T(8,128)(2,1)S(1)}, bf16[2560,512]{1,0:T(8,128)(2,1)}, u32[]{:S(2)}) copy-start(bf16[2560,512]{1,0:T(8,128)(2,1)} %all-gather.5.cloned.1.call-done) | copy-start | bytes 7864324
  636.8 10.4 %copy-start.33 = (f32[2560]{0:T(1024)S(1)}, f32[2560]{0:T(1024)}, u32[]{:S(2)}) copy-start(f32[2560]{0:T(1024)} %copy-done.32) | copy-start | bytes 30724
  636.8 10.4 %copy-start.35 = (f32[2560]{0:T(1024)S(1)}, f32[2560]{0:T(1024)}, u32[]{:S(2)}) copy-start(f32[2560]{0:T(1024)} %copy-done.34) | copy-start | bytes 30724
  636.8 10.4 %copy-start.41 = (f32[1,512]{1,0:T(1,128)S(1)}, f32[1,512]{1,0:T(1,128)}, u32[]{:S(2)}) copy-start(f32[1,512]{1,0:T(1,128)} %copy-done.40) | copy-start | bytes 6148
  636.8 10.4 %copy-start.50 = (f32[1,512]{1,0:T(1,128)S(1)}, f32[1,512]{1,0:T(1,128)}, u32[]{:S(2)}) copy-start(f32[1,512]{1,0:T(1,128)} %copy-done.49) | copy-start | bytes 6148
  652.8 173.5 %all-gather.9.cloned.1.call-start = ((), (), s32[]{:S(2)}) async-start(), calls=%async_computation.3 | async-start | bytes 7864320 | tf_op jit(solution)/shard_map/all_gather | solution.py:203
  837.4 76.0 %copy-start.11 = (f32[3,512,256]{1,2,0:T(8,128)S(1)}, f32[3,512,256]{1,2,0:T(8,128)}, u32[]{:S(2)}) copy-start(f32[3,512,256]{1,2,0:T(8,128)} %copy.95) | copy-start | bytes 4718596
  837.4 76.0 %copy-start.12 = (f32[3,512,256]{1,2,0:T(8,128)S(1)}, f32[3,512,256]{1,2,0:T(8,128)}, u32[]{:S(2)}) copy-start(f32[3,512,256]{1,2,0:T(8,128)} %copy.92) | copy-start | bytes 4718596
  918.1 9.2 copy-start.36
  918.1 9.2 copy-start.37
  918.2 9.8 %copy-start.19 = (f32[256,512]{1,0:T(8,128)S(1)}, f32[256,512]{1,0:T(8,128)}, u32[]{:S(2)}) copy-start(f32[256,512]{1,0:T(8,128)} %param.28) | copy-start | bytes 1572868
  918.2 9.8 %copy-start.30 = (bf16[256,512]{1,0:T(8,128)(2,1)S(1)}, bf16[256,512]{1,0:T(8,128)(2,1)}, u32[]{:S(2)}) copy-start(bf16[256,512]{1,0:T(8,128)(2,1)} %get-tuple-element.86) | copy-start | bytes 786436
  921.4 9.2 copy-start.21
  (40 other events, 200.9 us)
Sparse Core Ops, SparseCore 0:
  9.6 41.7 all-gather.4
  146.6 130.5 all-reduce.7
  278.8 39.0 all-gather.6
  339.9 130.8 all-reduce.11
  652.9 104.0 all-reduce.9
  759.0 67.2 all-gather.8
